TPU v7x, 32 devices: a whole 2x2x4 slice. The times are simulated.
32 devices in a mesh: groups: 2 (over y), side: 2 (over core), ffn: 4 (over z), rep: 2 (over x).
Axes of the slice: x: 2, y: 2, z: 4, core: 2. Of those that a mesh axis runs over, the one named last changes fastest.
Arguments:
- queries: bfloat16 [16, 8192], P(('groups', 'side', 'rep')), parts along dimension 0, may hold values from -24 to 24
- key_cache: bfloat16 [16, 3072, 1024], P(('groups', 'side', 'rep'), 'ffn'), parts along dimension 0, may hold values from -4 to 4
- value_cache: bfloat16 [16, 3072, 1024], P(('groups', 'side', 'rep'), 'ffn'), parts along dimension 0, may hold values from -24 to 24
- decoded_key: bfloat16 [16, 1024], P(('groups', 'side', 'rep')), parts along dimension 0, may hold values from -6 to 6
- decoded_value: bfloat16 [16, 1024], P(('groups', 'side', 'rep')), parts along dimension 0, may hold values from -24 to 24
- lengths: int32 [16], P(('groups', 'side', 'rep')), parts along dimension 0, may hold values from 2 to 3072, as said below
- counts: int32 [8], P('groups'), parts along dimension 0, may hold values from 1 to 2, as said below
- residual: bfloat16 [16, 8192], P('groups', ('side', 'ffn', 'rep')), parts along dimension 0, may hold values from -144 to 144
- out_weight: bfloat16 [8192, 8192], P(None, ('side', 'ffn', 'rep')), may hold values from -0.0625 to 0.0625
- norm_gain: bfloat16 [8192], P(('side', 'ffn', 'rep')), may hold values from 0.099609375 to 1.8984375
- gate_weight: bfloat16 [14336, 8192], P('rep', ('side', 'ffn')), may hold values from -0.0625 to 0.0625
- up_weight: bfloat16 [14336, 8192], P('rep', ('side', 'ffn')), may hold values from -0.0625 to 0.0625
- down_weight: bfloat16 [14336, 8192], P('rep', ('side', 'ffn')), may hold values from -0.046875 to 0.046875
Outputs:
- layer_out: bfloat16 [16, 8192], P('groups', ('side', 'ffn', 'rep')), parts along dimension 0
There are 2 independent parts, one for each index of `groups`. A program takes and returns all parts, laid end to end along the dimension named above; an argument that names none is the same for every part. Nothing has to cross between parts.
Inputs may be any that keep to these rules, and one draw needn't show every extreme that they name: `lengths`: a request's positions at or past its length are ignored; some request has all 3072 positions in use. `counts`: slots at or past a group's count are unused; some group uses all 2 slots.
All inputs are finite; a program needn't handle non-finite values.
Results may differ from a plain program's by a relative error of at most 0.014.
Values may be sent and summed in bfloat16 or wider, within the bound.
A program may use at most 128 MiB of HBM per device.

v0:
```python
import functools

import jax
import jax.numpy as jnp
from jax import lax
from jax.experimental import pallas as pl
from jax.experimental.pallas import tpu as pltpu
from jax.sharding import PartitionSpec as P

D = 8192
QUERY_HEADS = 64
KEY_VALUE_HEADS = 8
HEAD_WIDTH = 128
GROUP_WIDTH = QUERY_HEADS // KEY_VALUE_HEADS
OUT_CHUNKS = 4

norm_eps = 1e-05
MESH = pl.DeviceIdType.MESH
NT = (((1,), (1,)), ((), ()))
f32 = jnp.float32
bf16 = jnp.bfloat16


def kernel(
    S, F, R,
    q_ref, dk_ref, dv_ref, len_ref, cnt_ref, res_ref, gain_ref,
    k_hbm, v_hbm, wo_hbm, wg_hbm, wu_hbm, wd_hbm,
    out_ref,
    k_v, v_v, wo_v, wg_v, wu_v, wd_v,
    qbd, acc_buf, stat_buf, att_row, att_buf, att_full,
    y_buf, sq_rep, sq_buf, pre,
    gu_send_a, gu_recv_a, hid_a, gu_send_b, gu_recv_b, hid_b, d_send, d_recv,
    k_sem, v_sem, wo_sem, wg_sem, wu_sem, wd_sem,
    acc_ss, acc_rs, stat_ss, stat_rs, att_ss, att_rs,
    y_ss, y_rs, sqr_ss, sqr_rs, sq_ss, sq_rs,
    gu_ss_a, gu_rs_a, hid_ss_a, hid_rs_a, gu_ss_b, gu_rs_b, hid_ss_b, hid_rs_b, d_ss, d_rs,
):
    s = lax.axis_index("side")
    f = lax.axis_index("ffn")
    r = lax.axis_index("rep")
    PN = S * F
    SR = S * R
    me = s * F + f
    mine = s * R + r
    rows_q = q_ref.shape[0]
    span = k_v.shape[1]
    total_rows, cols = res_ref.shape
    kv_width = KEY_VALUE_HEADS * HEAD_WIDTH
    unit = wg_v.shape[1]
    seg_cols = wg_v.shape[2]
    out_rows = wo_v.shape[1]
    scale = HEAD_WIDTH ** (-0.5)

    def dev(side, ffn, rep):
        return {"side": side, "ffn": ffn, "rep": rep}

    def remote(src, dst, ss, rs, to):
        return pltpu.make_async_remote_copy(
            src_ref=src, dst_ref=dst, send_sem=ss, recv_sem=rs, device_id=to, device_id_type=MESH
        )

    def k_copy(i):
        return pltpu.make_async_copy(k_hbm.at[i], k_v.at[i], k_sem.at[i])

    def v_copy(i):
        return pltpu.make_async_copy(v_hbm.at[i], v_v.at[i], v_sem.at[i])

    def wo_copy(i):
        return pltpu.make_async_copy(
            wo_hbm.at[pl.ds(i * out_rows, out_rows)], wo_v.at[i], wo_sem.at[i]
        )

    def unit_copy(hbm, buf, sem, p):
        at = pl.multiple_of(p * unit, 8)
        return pltpu.make_async_copy(hbm.at[pl.ds(at, unit)], buf.at[p], sem.at[p])

    def far_first(t):
        off = F - 1 - t // S
        side = lax.rem(s + 1 + lax.rem(t, S), S)
        ffn = lax.rem(f + off, F)
        return side, ffn, side * F + ffn

    def near_first(t):
        side = lax.rem(s + lax.rem(t, S), S)
        ffn = lax.rem(f - t // S + F, F)
        return side, ffn, side * F + ffn

    for i in range(rows_q):
        k_copy(i).start()
    for i in range(rows_q):
        v_copy(i).start()
    for i in range(OUT_CHUNKS):
        wo_copy(i).start(priority=1)

    barrier = pltpu.get_barrier_semaphore()
    group = S * F * R
    my_id = me * R + r

    def greet(t, c):
        other = lax.rem(my_id + t, group)
        pl.semaphore_signal(
            barrier,
            inc=1,
            device_id=dev(other // (F * R), lax.rem(other // R, F), lax.rem(other, R)),
            device_id_type=MESH,
        )
        return c

    lax.fori_loop(1, group, greet, 0)

    qbd[...] = jnp.zeros(qbd.shape, f32)
    for i in range(rows_q):
        for h in range(QUERY_HEADS):
            b = h // GROUP_WIDTH
            qbd[i, h : h + 1, b * HEAD_WIDTH : (b + 1) * HEAD_WIDTH] = q_ref[
                i : i + 1, h * HEAD_WIDTH : (h + 1) * HEAD_WIDTH
            ].astype(f32)

    start_pos = f * span
    leading = f == 0
    positions = start_pos + lax.broadcasted_iota(jnp.int32, (QUERY_HEADS, span), 1)
    diag = (
        lax.broadcasted_iota(jnp.int32, (QUERY_HEADS, kv_width), 0) // GROUP_WIDTH
        == lax.broadcasted_iota(jnp.int32, (QUERY_HEADS, kv_width), 1) // HEAD_WIDTH
    )

    def acc_copy(to, slot, i):
        return remote(
            acc_buf.at[slot, i], acc_buf.at[slot, i], acc_ss.at[to, i], acc_rs.at[slot, i],
            dev(s, to, r),
        )

    def stat_copy(to, slot, i):
        return remote(
            stat_buf.at[slot, i], stat_buf.at[slot, i], stat_ss.at[to, i], stat_rs.at[slot, i],
            dev(s, to, r),
        )

    for i in range(rows_q):
        qf = qbd[i]
        fresh = (
            jnp.sum(qf * dk_ref[i : i + 1, :].astype(f32), axis=-1, keepdims=True) * scale
        )
        k_copy(i).wait()
        if i == rows_q - 1:
            def start_gu(t, c):
                _, _, p = far_first(t)
                unit_copy(wg_hbm, wg_v, wg_sem, p).start(priority=1)
                unit_copy(wu_hbm, wu_v, wu_sem, p).start(priority=1)
                return c

            lax.fori_loop(0, PN, start_gu, 0)
        sc = lax.dot_general(qf.astype(bf16), k_v[i], NT, preferred_element_type=f32) * scale
        in_range = positions < len_ref[i]
        peak = jnp.max(jnp.where(in_range, sc, -1e30), axis=-1, keepdims=True)
        peak = jnp.where(leading, jnp.maximum(peak, fresh), peak)
        w = jnp.where(in_range, jnp.exp(sc - peak), 0.0)
        wn = jnp.where(leading, jnp.exp(fresh - peak), 0.0)
        norm = jnp.sum(w, axis=-1, keepdims=True) + wn
        both = jnp.broadcast_to(jnp.concatenate([peak, norm], axis=0), (2 * QUERY_HEADS, 128))
        stat_buf[f, i] = both.T[0:8, :]
        v_copy(i).wait()
        o = jnp.dot(w.astype(bf16), v_v[i], preferred_element_type=f32)
        o = o + wn.astype(bf16).astype(f32) * dv_ref[i : i + 1, :].astype(f32)
        o = jnp.where(diag, o, 0.0)
        part = o[:, :HEAD_WIDTH]
        for b in range(1, KEY_VALUE_HEADS):
            part = part + o[:, b * HEAD_WIDTH : (b + 1) * HEAD_WIDTH]
        acc_buf[f, i] = part.astype(bf16)
        if i == 0:
            pl.semaphore_wait(barrier, group - 1)

        def send_acc(t, c, i=i):
            to = lax.rem(f + t, F)
            stat_copy(to, f, i).start()
            acc_copy(to, f, i).start()
            return c

        lax.fori_loop(1, F, send_acc, 0)

    def start_down(t, c):
        _, _, p = near_first(t)
        unit_copy(wd_hbm, wd_v, wd_sem, p).start(priority=1)
        return c

    lax.fori_loop(0, PN, start_down, 0)

    def att_copy(other, slot, i):
        return remote(
            att_buf.at[slot, i], att_buf.at[slot, i], att_ss.at[other, i], att_rs.at[slot, i],
            dev(other // R, f, lax.rem(other, R)),
        )

    low = lax.broadcasted_iota(jnp.int32, (8, 128), 1) < QUERY_HEADS
    for i in range(rows_q):
        def recv_acc(t, c, i=i):
            src = lax.rem(f + t, F)
            stat_copy(src, src, i).wait_recv()
            acc_copy(src, src, i).wait_recv()
            return c

        lax.fori_loop(1, F, recv_acc, 0)
        stats = [stat_buf[z, i] for z in range(F)]
        top = stats[0]
        for z in range(1, F):
            top = jnp.maximum(top, stats[z])
        factors = [jnp.exp(v - top) for v in stats]
        total = factors[0] * pltpu.roll(stats[0], QUERY_HEADS, 1)
        for z in range(1, F):
            total = total + factors[z] * pltpu.roll(stats[z], QUERY_HEADS, 1)
        total = jnp.where(low, total, 1.0)
        factors = [v / total for v in factors]
        if 8 * F < 128:
            factors.append(jnp.zeros((128 - 8 * F, 128), f32))
        turned = jnp.concatenate(factors, axis=0).T
        attended = turned[:QUERY_HEADS, 0:1] * acc_buf[0, i].astype(f32)
        for z in range(1, F):
            attended = attended + turned[:QUERY_HEADS, 8 * z : 8 * z + 1] * acc_buf[z, i].astype(f32)
        for h in range(QUERY_HEADS):
            att_row[i : i + 1, h * HEAD_WIDTH : (h + 1) * HEAD_WIDTH] = attended[h : h + 1, :]
        att_buf[mine, i] = att_row[i : i + 1, :].astype(bf16)

        def send_att(t, c, i=i):
            att_copy(lax.rem(mine + t, SR), mine, i).start()
            return c

        lax.fori_loop(1, SR, send_att, 0)

    def recv_att(t, c):
        src = lax.rem(mine + t, SR)
        for i in range(rows_q):
            att_copy(src, src, i).wait_recv()
        return c

    lax.fori_loop(1, SR, recv_att, 0)
    for j in range(SR):
        for i in range(rows_q):
            at = j * rows_q + i
            att_full[at : at + 1, :] = att_buf[j, i].astype(f32)
    proj = res_ref[...].astype(f32)
    summed = jnp.zeros((total_rows, cols), f32)
    for i in range(OUT_CHUNKS):
        wo_copy(i).wait()
        summed = summed + jnp.dot(
            att_full[:, i * out_rows : (i + 1) * out_rows].astype(bf16),
            wo_v[i],
            preferred_element_type=f32,
        )
    stream = (proj + summed).astype(bf16).astype(f32)
    y_buf[r] = (stream * gain_ref[...].astype(f32).reshape(1, cols)).astype(bf16)
    sq_rep[r] = jnp.broadcast_to(jnp.sum(stream * stream, axis=1, keepdims=True), (total_rows, 128))

    def y_copy(to, slot):
        return remote(y_buf.at[slot], y_buf.at[slot], y_ss.at[to], y_rs.at[slot], dev(s, f, to))

    def sqr_copy(to, slot):
        return remote(
            sq_rep.at[slot], sq_rep.at[slot], sqr_ss.at[to], sqr_rs.at[slot], dev(s, f, to)
        )

    def send_y(t, c):
        to = lax.rem(r + t, R)
        y_copy(to, r).start()
        sqr_copy(to, r).start()
        return c

    lax.fori_loop(1, R, send_y, 0)

    aligned = cols % 128 == 0
    parts = (
        (0, hid_a.shape[2], gu_send_a, gu_recv_a, gu_ss_a, gu_rs_a, hid_a, hid_ss_a, hid_rs_a),
        (hid_a.shape[2], hid_b.shape[2],
         gu_send_b, gu_recv_b, gu_ss_b, gu_rs_b, hid_b, hid_ss_b, hid_rs_b),
    )
    width_a = hid_a.shape[2]

    def half_of(t, which, lhs):
        _, _, p = far_first(t)
        at = pl.ds(pl.multiple_of(which * cols, 128), cols)
        g = lax.dot_general(lhs, wg_v[p, :width_a, at], NT, preferred_element_type=f32)
        u = lax.dot_general(lhs, wu_v[p, :width_a, at], NT, preferred_element_type=f32)
        return g, u

    early = pre.shape[0] if aligned and R == 2 else 0
    if early:
        own_y = y_buf[r]

        def ahead(t, c):
            _, _, p = far_first(t)
            unit_copy(wg_hbm, wg_v, wg_sem, p).wait()
            unit_copy(wu_hbm, wu_v, wu_sem, p).wait()
            g, u = half_of(t, r, own_y)
            pre[t, 0] = g
            pre[t, 1] = u
            return c

        lax.fori_loop(0, early, ahead, 0)

    def recv_y(t, c):
        src = lax.rem(r + t, R)
        y_copy(src, src).wait_recv()
        sqr_copy(src, src).wait_recv()
        return c

    lax.fori_loop(1, R, recv_y, 0)
    squares = sq_rep[0]
    for j in range(1, R):
        squares = squares + sq_rep[j]
    sq_buf[me] = squares

    def sq_copy(t, own):
        side, ffn, p = far_first(t)
        slot = me if own else p
        return remote(
            sq_buf.at[slot], sq_buf.at[slot], sq_ss.at[p], sq_rs.at[slot], dev(side, ffn, r)
        )

    def send_sq(t, c):
        sq_copy(t, True).start()
        return c

    lax.fori_loop(0, PN - 1, send_sq, 0)

    def place(j):
        a = lax.broadcasted_iota(jnp.int32, (cols, seg_cols), 0)
        b = lax.broadcasted_iota(jnp.int32, (cols, seg_cols), 1)
        return jnp.where(b == a + j * cols, 1.0, 0.0).astype(bf16)

    if aligned:
        segment = jnp.concatenate([y_buf[j] for j in range(R)], axis=1)
    else:
        segment = jnp.zeros((total_rows, seg_cols), f32)
        for j in range(R):
            segment = segment + jnp.dot(y_buf[j], place(j), preferred_element_type=f32)
        segment = segment.astype(bf16)

    def gu_copy(part, t, own):
        _, _, gu_send, gu_recv, gu_ss, gu_rs, _, _, _ = parts[part]
        side, ffn, p = far_first(t)
        slot = me if own else p
        return remote(
            gu_send.at[p], gu_recv.at[slot], gu_ss.at[p], gu_rs.at[slot], dev(side, ffn, r)
        )

    def hand_over(part, t, g, u):
        gu_send = parts[part][2]
        _, _, p = far_first(t)
        gu_send[p, 0] = g.astype(bf16)
        gu_send[p, 1] = u.astype(bf16)

        @pl.when(t < PN - 1)
        def _():
            gu_copy(part, t, True).start()

    if early:
        other_y = y_buf[1 - r]

        def finish(t, c):
            g, u = half_of(t, 1 - r, other_y)
            hand_over(0, t, g + pre[t, 0], u + pre[t, 1])
            return c

        lax.fori_loop(0, early, finish, 0)

    def project(part, wait):
        lo, width = parts[part][:2]

        def step(t, c):
            _, _, p = far_first(t)
            if wait:
                unit_copy(wg_hbm, wg_v, wg_sem, p).wait()
            g = lax.dot_general(segment, wg_v[p, lo : lo + width], NT, preferred_element_type=f32)
            if wait:
                unit_copy(wu_hbm, wu_v, wu_sem, p).wait()
            u = lax.dot_general(segment, wu_v[p, lo : lo + width], NT, preferred_element_type=f32)
            hand_over(part, t, g, u)
            return c

        return step

    def hid_copy(part, t, own):
        hid, hid_ss, hid_rs = parts[part][6:]
        side, ffn, p = far_first(t) if own else near_first(t)
        slot = me if own else p
        return remote(
            hid.at[slot], hid.at[slot], hid_ss.at[p], hid_rs.at[slot], dev(side, ffn, r)
        )

    def activate(part, factor):
        _, _, gu_send, gu_recv, _, _, hid, _, _ = parts[part]

        def gather_sums(t, c):
            g, u = c
            _, _, p = far_first(t)
            gu_copy(part, t, False).wait_recv()
            return g + gu_recv[p, 0].astype(f32), u + gu_recv[p, 1].astype(f32)

        g, u = lax.fori_loop(
            0, PN - 1, gather_sums, (gu_send[me, 0].astype(f32), gu_send[me, 1].astype(f32))
        )
        g = g * factor
        u = u * factor
        hid[me] = (g / (1.0 + jnp.exp(-g)) * u).astype(bf16)

        def send_hid(t, c):
            hid_copy(part, t, True).start()
            return c

        lax.fori_loop(0, PN - 1, send_hid, 0)

    lax.fori_loop(early, PN, project(0, True), 0)
    lax.fori_loop(0, PN // 2, project(1, False), 0)

    def gather_squares(t, c):
        _, _, p = far_first(t)
        sq_copy(t, False).wait_recv()
        return c + sq_buf[p]

    q = lax.fori_loop(0, PN - 1, gather_squares, sq_buf[me])
    factor = lax.rsqrt(q / D + norm_eps)[:, 0:1]
    activate(0, factor)
    lax.fori_loop(PN // 2, PN, project(1, False), 0)
    activate(1, factor)

    def down(part):
        lo, width = parts[part][:2]
        hid = parts[part][6]

        def step(t, c):
            _, _, p = near_first(t)
            if part == 0:
                unit_copy(wd_hbm, wd_v, wd_sem, p).wait()

            @pl.when(t > 0)
            def _():
                hid_copy(part, t, False).wait_recv()

            return c + jnp.dot(hid[p], wd_v[p, lo : lo + width], preferred_element_type=f32)

        return step

    terms = jnp.zeros((total_rows, seg_cols), f32)
    for part in range(2):
        terms = lax.fori_loop(0, PN, down(part), terms, unroll=True)
    terms = terms.astype(bf16)
    for j in range(R):
        if aligned:
            d_send[j] = terms[:, j * cols : (j + 1) * cols]
        else:
            d_send[j] = lax.dot_general(
                terms, place(j), NT, preferred_element_type=f32
            ).astype(bf16)

    def d_copy(to, own):
        return remote(
            d_send.at[to], d_recv.at[r if own else to], d_ss.at[to],
            d_rs.at[r if own else to], dev(s, f, to),
        )

    def send_d(t, c):
        d_copy(lax.rem(r + t, R), True).start()
        return c

    lax.fori_loop(1, R, send_d, 0)

    row = lax.broadcasted_iota(jnp.int32, (total_rows, cols), 0)
    slots = total_rows // cnt_ref.shape[0]
    limit = jnp.zeros((total_rows, cols), jnp.int32)
    for i in range(cnt_ref.shape[0]):
        limit = jnp.where(row // slots == i, cnt_ref[i], limit)
    active = lax.rem(row, slots) < limit

    def recv_d(t, c):
        src = lax.rem(r + t, R)
        d_copy(src, False).wait_recv()
        return c + d_recv[src].astype(f32)

    ffn_out = lax.fori_loop(1, R, recv_d, d_send[r].astype(f32))
    out_ref[...] = jnp.where(active, stream + ffn_out, 0.0).astype(bf16)

    def drain_f(t, c):
        to = lax.rem(f + t, F)
        for i in range(rows_q):
            stat_copy(to, f, i).wait_send()
            acc_copy(to, f, i).wait_send()
        return c

    lax.fori_loop(1, F, drain_f, 0)

    def drain_sr(t, c):
        for i in range(rows_q):
            att_copy(lax.rem(mine + t, SR), mine, i).wait_send()
        return c

    lax.fori_loop(1, SR, drain_sr, 0)

    def drain_r(t, c):
        to = lax.rem(r + t, R)
        y_copy(to, r).wait_send()
        sqr_copy(to, r).wait_send()
        d_copy(to, True).wait_send()
        return c

    lax.fori_loop(1, R, drain_r, 0)

    def drain_p(t, c):
        sq_copy(t, True).wait_send()
        for part in range(2):
            gu_copy(part, t, True).wait_send()
            hid_copy(part, t, True).wait_send()
        return c

    lax.fori_loop(0, PN - 1, drain_p, 0)


def body(S, F, R, queries, key_cache, value_cache, decoded_key, decoded_value, lengths, counts,
         residual, out_weight, norm_gain, gate_weight, up_weight, down_weight):
    rows_q = queries.shape[0]
    span = key_cache.shape[1]
    kv_width = key_cache.shape[2]
    total_rows, cols = residual.shape
    units, seg_cols = gate_weight.shape
    PN, SR = S * F, S * R
    unit = units // PN
    step = 128 if unit % 128 == 0 else 16
    width_a = unit * 4 // 7 // step * step
    widths = (width_a, unit - width_a)
    out_rows = out_weight.shape[0] // OUT_CHUNKS
    dma = pltpu.SemaphoreType.DMA
    vmem = pl.BlockSpec(memory_space=pltpu.VMEM)
    smem = pl.BlockSpec(memory_space=pltpu.SMEM)
    hbm = pl.BlockSpec(memory_space=pl.ANY)
    return pl.pallas_call(
        functools.partial(kernel, S, F, R),
        out_shape=jax.ShapeDtypeStruct((total_rows, cols), bf16),
        in_specs=[vmem, vmem, vmem, smem, smem, vmem, vmem] + [hbm] * 6,
        out_specs=vmem,
        scratch_shapes=[
            pltpu.VMEM((rows_q, span, kv_width), bf16),
            pltpu.VMEM((rows_q, span, kv_width), bf16),
            pltpu.VMEM((OUT_CHUNKS, out_rows, cols), bf16),
            pltpu.VMEM((PN, unit, seg_cols), bf16),
            pltpu.VMEM((PN, unit, seg_cols), bf16),
            pltpu.VMEM((PN, unit, seg_cols), bf16),
            pltpu.VMEM((rows_q, QUERY_HEADS, kv_width), f32),
            pltpu.VMEM((F, rows_q, QUERY_HEADS, HEAD_WIDTH), bf16),
            pltpu.VMEM((F, rows_q, 8, 128), f32),
            pltpu.VMEM((rows_q, QUERY_HEADS * HEAD_WIDTH), f32),
            pltpu.VMEM((SR, rows_q, 1, QUERY_HEADS * HEAD_WIDTH), bf16),
            pltpu.VMEM((total_rows, QUERY_HEADS * HEAD_WIDTH), f32),
            pltpu.VMEM((R, total_rows, cols), bf16),
            pltpu.VMEM((R, total_rows, 128), f32),
            pltpu.VMEM((PN, total_rows, 128), f32),
            pltpu.VMEM((PN // 2 + 1, 2, total_rows, width_a), f32),
            *[
                pltpu.VMEM(shape, bf16)
                for width in widths
                for shape in (
                    (PN, 2, total_rows, width), (PN, 2, total_rows, width),
                    (PN, total_rows, width),
                )
            ],
            pltpu.VMEM((R, total_rows, cols), bf16),
            pltpu.VMEM((R, total_rows, cols), bf16),
            dma((rows_q,)), dma((rows_q,)), dma((OUT_CHUNKS,)),
            dma((PN,)), dma((PN,)), dma((PN,)),
            dma((F, rows_q)), dma((F, rows_q)), dma((F, rows_q)), dma((F, rows_q)),
            dma((SR, rows_q)), dma((SR, rows_q)),
            dma((R,)), dma((R,)), dma((R,)), dma((R,)), dma((PN,)), dma((PN,)),
            *[dma((PN,)) for _ in range(8)], dma((R,)), dma((R,)),
        ],
        compiler_params=pltpu.CompilerParams(
            collective_id=0, has_side_effects=True, vmem_limit_bytes=67043328
        ),
        name="decode_step",
    )(queries, decoded_key, decoded_value, lengths, counts, residual,
      norm_gain, key_cache, value_cache, out_weight, gate_weight, up_weight,
      down_weight)


def solution(mesh):
    S, F, R = mesh.shape["side"], mesh.shape["ffn"], mesh.shape["rep"]
    return jax.shard_map(
        functools.partial(body, S, F, R),
        mesh=mesh,
        in_specs=(
            P(("groups", "side", "rep"), None),
            P(("groups", "side", "rep"), "ffn", None),
            P(("groups", "side", "rep"), "ffn", None),
            P(("groups", "side", "rep"), None),
            P(("groups", "side", "rep"), None),
            P(("groups", "side", "rep")),
            P("groups"),
            P("groups", ("side", "ffn", "rep")),
            P(None, ("side", "ffn", "rep")),
            P(("side", "ffn", "rep")),
            P("rep", ("side", "ffn")),
            P("rep", ("side", "ffn")),
            P("rep", ("side", "ffn")),
        ),
        out_specs=P("groups", ("side", "ffn", "rep")),
        check_vma=False,
    )
```

profile of v0, /device:TPU:0, one launch (start us, length us, event | category | flops | bytes accessed | tf_op | source)
XLA Modules:
  0.0 42.1 jit_solution(4290895881831359228)
XLA Ops:
  0.0 40.8 %decode_step.1 = bf16[8,512]{1,0:T(8,128)(2,1)} custom-call(bf16[2,8192]{1,0:T(2,128)(2,1)} %q_ref.1, bf16[2,1024]{1,0:T(2,128)(2,1)} %dk_ref.1, bf16[2,1024]{1,0:T(2,128)(2,1)} %dv_ref.1, s32[2]{0:T(128)} %len_ref.1, s32[4]{0:T(128)} %cnt_ref.1, bf16[8,512]{1,0:T(8,128)(2,1)} %res_ref.1, bf16[512]{0:T(512)(128)(2,1)} %gain_ref.1, ...), custom_call_target="tpu_custom_call" | custom-call | tf_op jit(solution)/shard_map/decode_step/pallas_call | solution.py:533
  40.8 1.3 %copy.15 = bf16[8,512]{1,0:T(8,128)(2,1)} copy(bf16[8,512]{1,0:T(8,128)(2,1)} %decode_step.1) | data formatting | bytes 16384
where the time goes:
time: 42.3 us; the launch traced here: 42.1 us
  Pallas kernels  40.8 us (96%)
  local copies, waits for them, and re-layouts  1.3 us (3%)
    pallas_call x1, Pallas kernels, body(): pl.pallas_call(functools.partial(kernel, S, F, R), out_shape=jax.ShapeDty...  40.8 us
    unnamed x1, local copies, waits for them, and re-layouts  1.3 us

commit v1 on v0

--- a/solution.py
+++ b/solution.py
@@ -532,7 +532,7 @@
     hbm = pl.BlockSpec(memory_space=pl.ANY)
     return pl.pallas_call(
         functools.partial(kernel, S, F, R),
-        out_shape=jax.ShapeDtypeStruct((total_rows, cols), bf16),
+        out_shape=pltpu.VMEM((total_rows, cols), bf16),
         in_specs=[vmem, vmem, vmem, smem, smem, vmem, vmem] + [hbm] * 6,
         out_specs=vmem,
         scratch_shapes=[
@@ -570,7 +570,7 @@
             *[dma((PN,)) for _ in range(8)], dma((R,)), dma((R,)),
         ],
         compiler_params=pltpu.CompilerParams(
-            collective_id=0, has_side_effects=True, vmem_limit_bytes=67043328
+            collective_id=0, has_side_effects=True, vmem_limit_bytes=65000000
         ),
         name="decode_step",
     )(queries, decoded_key, decoded_value, lengths, counts, residual,

time: 42.3 us -> 41 us (0.969)
  local copies, waits for them, and re-layouts: 1.3 us -> 0.6 us
  Pallas kernels: 40.8 us -> 40.2 us
    unnamed x1, local copies, waits for them, and re-layouts: 1.3 us -> 0.6 us
    pallas_call x1, Pallas kernels: 40.8 us -> 40.2 us  [body(): pl.pallas_call(functools.partial(kernel, S, F, R), out_shape=pltpu.VMEM((...]
where the time goes in v1:
time: 41 us; the launch traced here: 40.8 us
  Pallas kernels  40.2 us (98%)
  local copies, waits for them, and re-layouts  0.6 us (1%)
    pallas_call x1, Pallas kernels, body(): pl.pallas_call(functools.partial(kernel, S, F, R), out_shape=pltpu.VMEM((...  40.2 us

profile of v1, /device:TPU:0, one launch (start us, length us, event | category | flops | bytes accessed | tf_op | source)
XLA Modules:
  0.0 40.8 jit_solution(7682536373223055969)
XLA Ops:
  0.0 40.2 %decode_step.1 = bf16[8,512]{1,0:T(8,128)(2,1)S(1)} custom-call(bf16[2,8192]{1,0:T(2,128)(2,1)} %q_ref.1, bf16[2,1024]{1,0:T(2,128)(2,1)} %dk_ref.1, bf16[2,1024]{1,0:T(2,128)(2,1)} %dv_ref.1, s32[2]{0:T(128)} %len_ref.1, s32[4]{0:T(128)} %cnt_ref.1, bf16[8,512]{1,0:T(8,128)(2,1)} %res_ref.1, bf16[512]{0:T(512)(128)(2,1)} %gain_ref.1, ...), custom_call_target="tpu_custom_call" | custom-call | tf_op jit(solution)/shard_map/decode_step/pallas_call | solution.py:533
  40.2 0.6 %copy.15 = bf16[8,512]{1,0:T(8,128)(2,1)} copy(bf16[8,512]{1,0:T(8,128)(2,1)S(1)} %decode_step.1) | data formatting | bytes 16384

commit v2 on v1

v2 whole, which is shorter than its diff:
```python
import functools

import jax
import jax.numpy as jnp
from jax import lax
from jax.experimental import pallas as pl
from jax.experimental.pallas import tpu as pltpu
from jax.sharding import PartitionSpec as P

D = 8192
QUERY_HEADS = 64
KEY_VALUE_HEADS = 8
HEAD_WIDTH = 128
GROUP_WIDTH = QUERY_HEADS // KEY_VALUE_HEADS
OUT_CHUNKS = 4
TURN_COLS = 256
WO_AT = 2
TURNS = ((0, 2), (2, 5), (5, 7))

norm_eps = 1e-05
MESH = pl.DeviceIdType.MESH
NT = (((1,), (1,)), ((), ()))
f32 = jnp.float32
bf16 = jnp.bfloat16


def kernel(
    S, F, R,
    q_hbm, dk_hbm, dv_hbm, len_hbm, cnt_hbm, res_hbm, gain_hbm,
    k_hbm, v_hbm, wo_hbm, wg_hbm, wu_hbm, wd_hbm,
    out_ref,
    q_ref, dk_ref, dv_ref, len_ref, cnt_ref, res_ref, gain_ref,
    k_v, v_v, wo_v, wt_v, wd_v,
    qbd, acc_buf, stat_buf, att_row, att_buf, att_full,
    y_buf,
    sib_send, sib_recv, gu_send, gu_recv, hid, d_send, d_recv,
    small_sem, k_sem, v_sem, wo_sem, raw_sem, wd_sem,
    acc_ss, acc_rs, stat_ss, stat_rs, att_ss, att_rs,
    y_ss, y_rs,
    sib_ss, sib_rs, gu_ss, gu_rs, hid_ss, hid_rs, d_ss, d_rs,
):
    s = lax.axis_index("side")
    f = lax.axis_index("ffn")
    r = lax.axis_index("rep")
    PN = S * F
    SR = S * R
    me = s * F + f
    mine = s * R + r
    rows_q = q_ref.shape[0]
    span = k_v.shape[1]
    total_rows, cols = res_ref.shape
    kv_width = KEY_VALUE_HEADS * HEAD_WIDTH
    unit, seg_cols = wd_v.shape[1:]
    turn = unit % 128 == 0 and seg_cols % 128 == 0
    pair = gu_recv.shape[2] - 128
    up_at = pair // 2
    ahead = PN // 2
    out_rows = wo_v.shape[1]
    scale = HEAD_WIDTH ** (-0.5)

    def dev(side, ffn, rep):
        return {"side": side, "ffn": ffn, "rep": rep}

    def remote(src, dst, ss, rs, to):
        return pltpu.make_async_remote_copy(
            src_ref=src, dst_ref=dst, send_sem=ss, recv_sem=rs, device_id=to, device_id_type=MESH
        )

    def k_copy(i):
        return pltpu.make_async_copy(k_hbm.at[i], k_v.at[i], k_sem.at[i])

    def v_copy(i):
        return pltpu.make_async_copy(v_hbm.at[i], v_v.at[i], v_sem.at[i])

    def wo_copy(i):
        return pltpu.make_async_copy(
            wo_hbm.at[pl.ds(i * out_rows, out_rows)], wo_v.at[i], wo_sem.at[i]
        )

    def unit_rows(p):
        return pl.ds(pl.multiple_of(p * unit, 8), unit)

    def wd_copy(p):
        return pltpu.make_async_copy(wd_hbm.at[unit_rows(p)], wd_v.at[p], wd_sem.at[p])

    def line(j):
        flip = 2 * f // F
        up = j + (j - f + F) // F
        v = F - 1 - j
        down = v - (f - v + F) // F
        last = (j + 1) // F
        return (1 - last) * (flip * up + (1 - flip) * down) + last * f

    def block(own, j):
        side = own * s + (1 - own) * (S - 1 - s)
        ffn = line(j)
        return side, ffn, side * F + ffn

    def in_turn(q):
        last = (q + 1) // PN
        own = (1 - lax.rem(q, 2)) * ((q + PN - 1) // PN) + last
        return block(own, own * (q // 2 - 1 + last) + (1 - own) * ((q + 1) // 2))

    def raw_copy(m, t):
        _, _, p = in_turn(t)
        src = (wg_hbm, wu_hbm)[m].at[unit_rows(p)]
        if turn:
            at = 2 * lax.rem(t, ahead) + m
            return pltpu.make_async_copy(src, wd_v.at[at], raw_sem.at[at])
        return pltpu.make_async_copy(src, wt_v.at[p, pl.ds(m * up_at, unit)], raw_sem.at[2 * t + m])

    def turn_pair(t, c):
        _, _, p = in_turn(t)
        for m in range(2):
            raw_copy(m, t).wait()
            for at in range(0, seg_cols, TURN_COLS):
                wt_v[p, at : at + TURN_COLS, m * up_at : m * up_at + unit] = wd_v[
                    2 * lax.rem(t, ahead) + m, :, at : at + TURN_COLS
                ].T

            @pl.when(t < PN - ahead)
            def _():
                raw_copy(m, t + ahead).start(priority=1)

            @pl.when(t >= PN - ahead)
            def _():
                wd_copy(2 * lax.rem(t, ahead) + m).start(priority=1)

        return c

    def turn_range(lo, hi):
        if turn:
            lax.fori_loop(lo * PN // 8, min(hi * PN // 8, PN - 1), turn_pair, 0)

    def far_first(t):
        last = t // (PN - 2)
        side = (1 - last) * lax.rem(t, 2) + last * (S - 1 - s)
        ffn = line(t // 2)
        return side, ffn, side * F + ffn

    def near_first(t):
        return block(1 - lax.rem(t, 2), F - 1 - t // 2)

    small = [
        pltpu.make_async_copy(src, dst, small_sem.at[n])
        for n, (src, dst) in enumerate((
            (q_hbm, q_ref), (dk_hbm, dk_ref), (dv_hbm, dv_ref), (len_hbm, len_ref),
            (cnt_hbm, cnt_ref), (res_hbm, res_ref), (gain_hbm, gain_ref),
        ))
    ]
    small[0].start()
    k_copy(0).start()
    for copy in small[1:4]:
        copy.start()
    for i in range(1, rows_q):
        k_copy(i).start()
    for i in range(rows_q):
        v_copy(i).start()
    for copy in small[4:]:
        copy.start()
    barrier = pltpu.get_barrier_semaphore()
    group = S * F * R
    my_id = me * R + r

    def greet(t, c):
        other = lax.rem(my_id + t, group)
        pl.semaphore_signal(
            barrier,
            inc=1,
            device_id=dev(other // (F * R), lax.rem(other // R, F), lax.rem(other, R)),
            device_id_type=MESH,
        )
        return c

    lax.fori_loop(1, group, greet, 0)

    qbd[...] = jnp.zeros(qbd.shape, f32)
    for copy in small[:4]:
        copy.wait()
    for i in range(rows_q):
        for h in range(QUERY_HEADS):
            b = h // GROUP_WIDTH
            qbd[i, h : h + 1, b * HEAD_WIDTH : (b + 1) * HEAD_WIDTH] = q_ref[
                i : i + 1, h * HEAD_WIDTH : (h + 1) * HEAD_WIDTH
            ].astype(f32)

    start_pos = f * span
    leading = f == 0
    positions = start_pos + lax.broadcasted_iota(jnp.int32, (QUERY_HEADS, span), 1)
    diag = (
        lax.broadcasted_iota(jnp.int32, (QUERY_HEADS, kv_width), 0) // GROUP_WIDTH
        == lax.broadcasted_iota(jnp.int32, (QUERY_HEADS, kv_width), 1) // HEAD_WIDTH
    )

    def acc_copy(to, slot, i):
        return remote(
            acc_buf.at[slot, i], acc_buf.at[slot, i], acc_ss.at[to, i], acc_rs.at[slot, i],
            dev(s, to, r),
        )

    def stat_copy(to, slot, i):
        return remote(
            stat_buf.at[slot, i], stat_buf.at[slot, i], stat_ss.at[to, i], stat_rs.at[slot, i],
            dev(s, to, r),
        )

    for i in range(rows_q):
        qf = qbd[i]
        fresh = (
            jnp.sum(qf * dk_ref[i : i + 1, :].astype(f32), axis=-1, keepdims=True) * scale
        )
        k_copy(i).wait()
        if i == rows_q - 1:
            def start_gu(t, c):
                raw_copy(0, t).start(priority=1)
                raw_copy(1, t).start(priority=1)
                return c

            lax.fori_loop(0, WO_AT if turn else PN, start_gu, 0)
            for n in range(OUT_CHUNKS):
                wo_copy(n).start(priority=1)
            lax.fori_loop(WO_AT if turn else PN, ahead if turn else PN, start_gu, 0)
        sc = lax.dot_general(qf.astype(bf16), k_v[i], NT, preferred_element_type=f32) * scale
        in_range = positions < len_ref[i]
        peak = jnp.max(jnp.where(in_range, sc, -1e30), axis=-1, keepdims=True)
        peak = jnp.where(leading, jnp.maximum(peak, fresh), peak)
        w = jnp.where(in_range, jnp.exp(sc - peak), 0.0)
        wn = jnp.where(leading, jnp.exp(fresh - peak), 0.0)
        norm = jnp.sum(w, axis=-1, keepdims=True) + wn
        both = jnp.broadcast_to(jnp.concatenate([peak, norm], axis=0), (2 * QUERY_HEADS, 128))
        stat_buf[f, i] = both.T[0:8, :]
        v_copy(i).wait()
        o = jnp.dot(w.astype(bf16), v_v[i], preferred_element_type=f32)
        o = o + wn.astype(bf16).astype(f32) * dv_ref[i : i + 1, :].astype(f32)
        o = jnp.where(diag, o, 0.0)
        part = o[:, :HEAD_WIDTH]
        for b in range(1, KEY_VALUE_HEADS):
            part = part + o[:, b * HEAD_WIDTH : (b + 1) * HEAD_WIDTH]
        acc_buf[f, i] = part.astype(bf16)
        if i == 0:
            pl.semaphore_wait(barrier, group - 1)

        def send_acc(t, c, i=i):
            to = lax.rem(f + t, F)
            stat_copy(to, f, i).start()
            acc_copy(to, f, i).start()
            return c

        lax.fori_loop(1, F, send_acc, 0)

    if not turn:
        def start_down(t, c):
            _, _, p = near_first(t)
            wd_copy(p).start(priority=1)
            return c

        lax.fori_loop(0, PN, start_down, 0)

    turn_range(*TURNS[0])

    def att_copy(other, slot, i):
        return remote(
            att_buf.at[slot, i], att_buf.at[slot, i], att_ss.at[other, i], att_rs.at[slot, i],
            dev(other // R, f, lax.rem(other, R)),
        )

    low = lax.broadcasted_iota(jnp.int32, (8, 128), 1) < QUERY_HEADS
    for i in range(rows_q):
        def recv_acc(t, c, i=i):
            src = lax.rem(f + t, F)
            stat_copy(src, src, i).wait_recv()
            acc_copy(src, src, i).wait_recv()
            return c

        lax.fori_loop(1, F, recv_acc, 0)
        stats = [stat_buf[z, i] for z in range(F)]
        top = stats[0]
        for z in range(1, F):
            top = jnp.maximum(top, stats[z])
        factors = [jnp.exp(v - top) for v in stats]
        total = factors[0] * pltpu.roll(stats[0], QUERY_HEADS, 1)
        for z in range(1, F):
            total = total + factors[z] * pltpu.roll(stats[z], QUERY_HEADS, 1)
        total = jnp.where(low, total, 1.0)
        factors = [v / total for v in factors]
        if 8 * F < 128:
            factors.append(jnp.zeros((128 - 8 * F, 128), f32))
        turned = jnp.concatenate(factors, axis=0).T
        attended = turned[:QUERY_HEADS, 0:1] * acc_buf[0, i].astype(f32)
        for z in range(1, F):
            attended = attended + turned[:QUERY_HEADS, 8 * z : 8 * z + 1] * acc_buf[z, i].astype(f32)
        for h in range(QUERY_HEADS):
            att_row[i : i + 1, h * HEAD_WIDTH : (h + 1) * HEAD_WIDTH] = attended[h : h + 1, :]
        att_buf[mine, i] = att_row[i : i + 1, :].astype(bf16)

        def send_att(t, c, i=i):
            att_copy(lax.rem(mine + t, SR), mine, i).start()
            return c

        lax.fori_loop(1, SR, send_att, 0)

    turn_range(*TURNS[1])

    def recv_att(t, c):
        src = lax.rem(mine + t, SR)
        for i in range(rows_q):
            att_copy(src, src, i).wait_recv()
        return c

    lax.fori_loop(1, SR, recv_att, 0)
    for j in range(SR):
        for i in range(rows_q):
            at = j * rows_q + i
            att_full[at : at + 1, :] = att_buf[j, i].astype(f32)
    for copy in small[4:]:
        copy.wait()
    proj = res_ref[...].astype(f32)
    summed = jnp.zeros((total_rows, cols), f32)
    for i in range(OUT_CHUNKS):
        wo_copy(i).wait()
        summed = summed + jnp.dot(
            att_full[:, i * out_rows : (i + 1) * out_rows].astype(bf16),
            wo_v[i],
            preferred_element_type=f32,
        )
    stream = (proj + summed).astype(bf16).astype(f32)
    lower = lax.broadcasted_iota(jnp.int32, (total_rows, 128), 1) < 64

    def split(v):
        high = v.astype(bf16).astype(f32)
        return jnp.where(lower, high, v - high).astype(bf16)

    def joined(v):
        v = v.astype(f32)
        return v + pltpu.roll(v, 64, 1)

    sq_at = y_buf.shape[2] - 128
    y_buf[r, :, :cols] = (stream * gain_ref[...].astype(f32).reshape(1, cols)).astype(bf16)
    y_buf[r, :, sq_at:] = split(
        jnp.broadcast_to(jnp.sum(stream * stream, axis=1, keepdims=True), (total_rows, 128))
    )

    def y_copy(to, slot):
        return remote(y_buf.at[slot], y_buf.at[slot], y_ss.at[to], y_rs.at[slot], dev(s, f, to))

    def send_y(t, c):
        to = lax.rem(r + t, R)
        y_copy(to, r).start()
        return c

    lax.fori_loop(1, R, send_y, 0)

    aligned = cols % 128 == 0
    turn_range(*TURNS[2])

    def recv_y(t, c):
        src = lax.rem(r + t, R)
        y_copy(src, src).wait_recv()
        return c

    lax.fori_loop(1, R, recv_y, 0)
    squares = joined(y_buf[0, :, sq_at:])
    for j in range(1, R):
        squares = squares + joined(y_buf[j, :, sq_at:])

    def place(j):
        a = lax.broadcasted_iota(jnp.int32, (cols, seg_cols), 0)
        b = lax.broadcasted_iota(jnp.int32, (cols, seg_cols), 1)
        return jnp.where(b == a + j * cols, 1.0, 0.0).astype(bf16)

    if aligned:
        segment = jnp.concatenate([y_buf[j, :, :cols] for j in range(R)], axis=1)
    else:
        segment = jnp.zeros((total_rows, seg_cols), f32)
        for j in range(R):
            segment = segment + jnp.dot(y_buf[j, :, :cols], place(j), preferred_element_type=f32)
        segment = segment.astype(bf16)

    def sib_copy(j):
        ffn = line(j)
        return remote(
            sib_send.at[ffn], sib_recv.at[ffn], sib_ss.at[ffn], sib_rs.at[ffn], dev(S - 1 - s, f, r)
        )

    def gu_copy(ffn, own):
        slot = f if own else ffn
        return remote(
            gu_send.at[ffn], gu_recv.at[slot], gu_ss.at[ffn], gu_rs.at[slot], dev(s, ffn, r)
        )

    def hid_copy(t, own):
        side, ffn, p = far_first(t) if own else near_first(t)
        slot = me if own else p
        return remote(
            hid.at[slot], hid.at[slot], hid_ss.at[p], hid_rs.at[slot], dev(side, ffn, r)
        )

    def project(p):
        if turn:
            return sum(
                jnp.dot(segment[:, at : at + 256], wt_v[p, at : at + 256], preferred_element_type=f32)
                for at in range(0, seg_cols, 256)
            )
        return lax.dot_general(segment, wt_v[p], NT, preferred_element_type=f32)

    def wait_raw(q):
        if not turn:
            raw_copy(0, q).wait()
            raw_copy(1, q).wait()

    def project_sibling(j):
        _, ffn, p = block(0, j)
        sib_send[ffn, :, :pair] = project(p).astype(bf16)
        sib_send[ffn, :, pair:] = split(squares)
        sib_copy(j).start()

    def project_far(j):
        _, ffn, p = block(1, j)
        v = project(p)
        sib_copy(j).wait_recv()
        gu_send[ffn, :, :pair] = (v + sib_recv[ffn, :, :pair].astype(f32)).astype(bf16)
        gu_send[ffn, :, pair:] = split(squares + joined(sib_recv[ffn, :, pair:]))
        gu_copy(ffn, True).start()

    def project_both(j, c):
        wait_raw(2 * j + 1)
        project_sibling(j + 1)
        wait_raw(2 * j + 2)
        project_far(j)
        return c

    wait_raw(0)
    project_sibling(0)
    lax.fori_loop(0, F - 1, project_both, 0)
    if turn:
        sums = []
        for m in range(2):
            at = 2 * lax.rem(PN - 1, ahead) + m
            raw_copy(m, PN - 1).wait()
            sums.append(
                lax.dot_general(segment, wd_v[at], NT, preferred_element_type=f32)
            )
            wd_copy(at).start(priority=1)
        sums = jnp.concatenate(sums, axis=1)
    else:
        wait_raw(PN - 1)
        sums = project(me)
    sib_copy(F - 1).wait_recv()
    sums = sums + sib_recv[f, :, :pair].astype(f32)
    squares = squares + joined(sib_recv[f, :, pair:])

    def gather_sums(t, c):
        src = line(F - 1 - t)
        gu_copy(src, False).wait_recv()
        v = gu_recv[src]
        return c[0] + v[:, :pair].astype(f32), c[1] + joined(v[:, pair:])

    sums, squares = lax.fori_loop(1, F, gather_sums, (sums, squares))
    sums = sums * lax.rsqrt(squares / D + norm_eps)[:, 0:1]
    g = sums[:, :unit]
    u = sums[:, up_at : up_at + unit]
    hid[me] = (g / (1.0 + jnp.exp(-g)) * u).astype(bf16)

    def send_hid(t, c):
        hid_copy(t, True).start()
        return c

    lax.fori_loop(0, PN - 1, send_hid, 0)

    def down(t, c):
        _, _, p = near_first(t)
        wd_copy(p).wait()

        @pl.when(t > 0)
        def _():
            hid_copy(t, False).wait_recv()

        return c + jnp.dot(hid[p], wd_v[p], preferred_element_type=f32)

    terms = jnp.zeros((total_rows, seg_cols), f32)
    terms = lax.fori_loop(0, PN, down, terms, unroll=True)
    terms = terms.astype(bf16)
    for j in range(R):
        if aligned:
            d_send[j] = terms[:, j * cols : (j + 1) * cols]
        else:
            d_send[j] = lax.dot_general(
                terms, place(j), NT, preferred_element_type=f32
            ).astype(bf16)

    def d_copy(to, own):
        return remote(
            d_send.at[to], d_recv.at[r if own else to], d_ss.at[to],
            d_rs.at[r if own else to], dev(s, f, to),
        )

    def send_d(t, c):
        d_copy(lax.rem(r + t, R), True).start()
        return c

    lax.fori_loop(1, R, send_d, 0)

    row = lax.broadcasted_iota(jnp.int32, (total_rows, cols), 0)
    slots = total_rows // cnt_ref.shape[0]
    limit = jnp.zeros((total_rows, cols), jnp.int32)
    for i in range(cnt_ref.shape[0]):
        limit = jnp.where(row // slots == i, cnt_ref[i], limit)
    active = lax.rem(row, slots) < limit

    def recv_d(t, c):
        src = lax.rem(r + t, R)
        d_copy(src, False).wait_recv()
        return c + d_recv[src].astype(f32)

    ffn_out = lax.fori_loop(1, R, recv_d, d_send[r].astype(f32))
    out_ref[...] = jnp.where(active, stream + ffn_out, 0.0).astype(bf16)

    def drain_f(t, c):
        to = lax.rem(f + t, F)
        for i in range(rows_q):
            stat_copy(to, f, i).wait_send()
            acc_copy(to, f, i).wait_send()
        return c

    lax.fori_loop(1, F, drain_f, 0)

    def drain_sr(t, c):
        for i in range(rows_q):
            att_copy(lax.rem(mine + t, SR), mine, i).wait_send()
        return c

    lax.fori_loop(1, SR, drain_sr, 0)

    def drain_r(t, c):
        to = lax.rem(r + t, R)
        y_copy(to, r).wait_send()
        d_copy(to, True).wait_send()
        return c

    lax.fori_loop(1, R, drain_r, 0)

    def drain_p(t, c):
        hid_copy(t, True).wait_send()
        return c

    lax.fori_loop(0, PN - 1, drain_p, 0)

    def drain_sibling(j, c):
        sib_copy(j).wait_send()
        return c

    lax.fori_loop(0, F, drain_sibling, 0)

    def drain_gu(t, c):
        gu_copy(lax.rem(f + t, F), True).wait_send()
        return c

    lax.fori_loop(1, F, drain_gu, 0)


def body(S, F, R, queries, key_cache, value_cache, decoded_key, decoded_value, lengths, counts,
         residual, out_weight, norm_gain, gate_weight, up_weight, down_weight):
    rows_q = queries.shape[0]
    span = key_cache.shape[1]
    kv_width = key_cache.shape[2]
    total_rows, cols = residual.shape
    units, seg_cols = gate_weight.shape
    PN, SR = S * F, S * R
    unit = units // PN
    turn = unit % 128 == 0 and seg_cols % 128 == 0
    pair = 2 * pl.cdiv(unit, 128) * 128
    turned = (seg_cols, pair) if turn else (pair, seg_cols)
    out_rows = out_weight.shape[0] // OUT_CHUNKS
    dma = pltpu.SemaphoreType.DMA
    vmem = pl.BlockSpec(memory_space=pltpu.VMEM)
    hbm = pl.BlockSpec(memory_space=pltpu.HBM)
    return pl.pallas_call(
        functools.partial(kernel, S, F, R),
        out_shape=pltpu.VMEM((total_rows, cols), bf16),
        in_specs=[hbm] * 13,
        out_specs=vmem,
        scratch_shapes=[
            pltpu.VMEM(queries.shape, bf16), pltpu.VMEM(decoded_key.shape, bf16),
            pltpu.VMEM(decoded_value.shape, bf16),
            pltpu.SMEM(lengths.shape, jnp.int32), pltpu.SMEM(counts.shape, jnp.int32),
            pltpu.VMEM(residual.shape, bf16), pltpu.VMEM(norm_gain.shape, bf16),
            pltpu.VMEM((rows_q, span, kv_width), bf16),
            pltpu.VMEM((rows_q, span, kv_width), bf16),
            pltpu.VMEM((OUT_CHUNKS, out_rows, cols), bf16),
            pltpu.VMEM((PN, *turned), bf16),
            pltpu.VMEM((PN, unit, seg_cols), bf16),
            pltpu.VMEM((rows_q, QUERY_HEADS, kv_width), f32),
            pltpu.VMEM((F, rows_q, QUERY_HEADS, HEAD_WIDTH), bf16),
            pltpu.VMEM((F, rows_q, 8, 128), f32),
            pltpu.VMEM((rows_q, QUERY_HEADS * HEAD_WIDTH), f32),
            pltpu.VMEM((SR, rows_q, 1, QUERY_HEADS * HEAD_WIDTH), bf16),
            pltpu.VMEM((total_rows, QUERY_HEADS * HEAD_WIDTH), f32),
            pltpu.VMEM((R, total_rows, pl.cdiv(cols, 128) * 128 + 128), bf16),
            *[pltpu.VMEM((F, total_rows, pair + 128), bf16) for _ in range(4)],
            pltpu.VMEM((PN, total_rows, unit), bf16),
            pltpu.VMEM((R, total_rows, cols), bf16),
            pltpu.VMEM((R, total_rows, cols), bf16),
            dma((7,)), dma((rows_q,)), dma((rows_q,)), dma((OUT_CHUNKS,)),
            dma((2 * PN,)), dma((PN,)),
            dma((F, rows_q)), dma((F, rows_q)), dma((F, rows_q)), dma((F, rows_q)),
            dma((SR, rows_q)), dma((SR, rows_q)),
            dma((R,)), dma((R,)), dma((F,)), dma((F,)), dma((F,)), dma((F,)), dma((PN,)), dma((PN,)),
            dma((R,)), dma((R,)),
        ],
        compiler_params=pltpu.CompilerParams(
            collective_id=0, has_side_effects=True, vmem_limit_bytes=65000000
        ),
        name="decode_step",
    )(queries, decoded_key, decoded_value, lengths, counts, residual,
      norm_gain, key_cache, value_cache, out_weight, gate_weight, up_weight,
      down_weight)


def solution(mesh):
    S, F, R = mesh.shape["side"], mesh.shape["ffn"], mesh.shape["rep"]
    return jax.shard_map(
        functools.partial(body, S, F, R),
        mesh=mesh,
        in_specs=(
            P(("groups", "side", "rep"), None),
            P(("groups", "side", "rep"), "ffn", None),
            P(("groups", "side", "rep"), "ffn", None),
            P(("groups", "side", "rep"), None),
            P(("groups", "side", "rep"), None),
            P(("groups", "side", "rep")),
            P("groups"),
            P("groups", ("side", "ffn", "rep")),
            P(None, ("side", "ffn", "rep")),
            P(("side", "ffn", "rep")),
            P("rep", ("side", "ffn")),
            P("rep", ("side", "ffn")),
            P("rep", ("side", "ffn")),
        ),
        out_specs=P("groups", ("side", "ffn", "rep")),
        check_vma=False,
    )
```

time: 41 us -> 38.1 us (0.929)
  Pallas kernels: 40.2 us -> 37.3 us
    pallas_call x1, Pallas kernels: 40.2 us -> 37.3 us  [body(): pl.pallas_call(functools.partial(kernel, S, F, R), out_shape=pltpu.VMEM((...]
where the time goes in v2:
time: 38.1 us; the launch traced here: 37.9 us
  Pallas kernels  37.3 us (98%)
  local copies, waits for them, and re-layouts  0.6 us (2%)
    pallas_call x1, Pallas kernels, body(): pl.pallas_call(functools.partial(kernel, S, F, R), out_shape=pltpu.VMEM((...  37.3 us

profile of v2, /device:TPU:0, one launch (start us, length us, event | category | flops | bytes accessed | tf_op | source)
XLA Modules:
  0.0 37.9 jit_solution(13247219336194117237)
XLA Ops:
  0.0 37.3 %decode_step.1 = bf16[8,512]{1,0:T(8,128)(2,1)S(1)} custom-call(bf16[2,8192]{1,0:T(2,128)(2,1)} %q_hbm.1, bf16[2,1024]{1,0:T(2,128)(2,1)} %dk_hbm.1, bf16[2,1024]{1,0:T(2,128)(2,1)} %dv_hbm.1, s32[2]{0:T(128)} %len_hbm.1, s32[4]{0:T(128)} %cnt_hbm.1, bf16[8,512]{1,0:T(8,128)(2,1)} %res_hbm.1, bf16[512]{0:T(512)(128)(2,1)} %gain_hbm.1, ...), custom_call_target="tpu_custom_call" | custom-call | tf_op jit(solution)/shard_map/decode_step/pallas_call | solution.py:577
  37.3 0.6 %copy.15 = bf16[8,512]{1,0:T(8,128)(2,1)} copy(bf16[8,512]{1,0:T(8,128)(2,1)S(1)} %decode_step.1) | data formatting | bytes 16384

commit v3 on v2

--- a/solution.py
+++ b/solution.py
@@ -31,7 +31,7 @@
     out_ref,
     q_ref, dk_ref, dv_ref, len_ref, cnt_ref, res_ref, gain_ref,
     k_v, v_v, wo_v, wt_v, wd_v,
-    qbd, acc_buf, stat_buf, att_row, att_buf, att_full,
+    q_rows, qbd, acc_buf, stat_buf, att_rows, att_buf, att_full,
     y_buf,
     sib_send, sib_recv, gu_send, gu_recv, hid, d_send, d_recv,
     small_sem, k_sem, v_sem, wo_sem, raw_sem, wd_sem,
@@ -174,23 +174,24 @@
 
     lax.fori_loop(1, group, greet, 0)
 
-    qbd[...] = jnp.zeros(qbd.shape, f32)
+    qbd[...] = jnp.zeros(qbd.shape, bf16)
     for copy in small[:4]:
         copy.wait()
-    for i in range(rows_q):
-        for h in range(QUERY_HEADS):
-            b = h // GROUP_WIDTH
-            qbd[i, h : h + 1, b * HEAD_WIDTH : (b + 1) * HEAD_WIDTH] = q_ref[
-                i : i + 1, h * HEAD_WIDTH : (h + 1) * HEAD_WIDTH
-            ].astype(f32)
+    for h in range(QUERY_HEADS):
+        pair_of = q_ref[:, h * HEAD_WIDTH : (h + 1) * HEAD_WIDTH].astype(f32)
+        for i in range(rows_q):
+            q_rows[i, h : h + 1, :] = pair_of[i : i + 1, :]
 
     start_pos = f * span
     leading = f == 0
-    positions = start_pos + lax.broadcasted_iota(jnp.int32, (QUERY_HEADS, span), 1)
-    diag = (
-        lax.broadcasted_iota(jnp.int32, (QUERY_HEADS, kv_width), 0) // GROUP_WIDTH
-        == lax.broadcasted_iota(jnp.int32, (QUERY_HEADS, kv_width), 1) // HEAD_WIDTH
-    )
+    positions = start_pos + lax.broadcasted_iota(jnp.int32, (1, span), 1)
+    heads = [
+        (slice(b * GROUP_WIDTH, (b + 1) * GROUP_WIDTH), slice(b * HEAD_WIDTH, (b + 1) * HEAD_WIDTH))
+        for b in range(KEY_VALUE_HEADS)
+    ]
+    for i in range(rows_q):
+        for at, lanes in heads:
+            qbd[i, at, lanes] = q_rows[i, at, :].astype(bf16)
 
     def acc_copy(to, slot, i):
         return remote(
@@ -205,9 +206,12 @@
         )
 
     for i in range(rows_q):
-        qf = qbd[i]
-        fresh = (
-            jnp.sum(qf * dk_ref[i : i + 1, :].astype(f32), axis=-1, keepdims=True) * scale
+        fresh = scale * jnp.concatenate(
+            [
+                jnp.sum(q_rows[i, at, :] * dk_ref[i : i + 1, lanes].astype(f32), axis=-1, keepdims=True)
+                for at, lanes in heads
+            ],
+            axis=0,
         )
         k_copy(i).wait()
         if i == rows_q - 1:
@@ -220,23 +224,22 @@
             for n in range(OUT_CHUNKS):
                 wo_copy(n).start(priority=1)
             lax.fori_loop(WO_AT if turn else PN, ahead if turn else PN, start_gu, 0)
-        sc = lax.dot_general(qf.astype(bf16), k_v[i], NT, preferred_element_type=f32) * scale
-        in_range = positions < len_ref[i]
-        peak = jnp.max(jnp.where(in_range, sc, -1e30), axis=-1, keepdims=True)
+        sc = lax.dot_general(qbd[i], k_v[i], NT, preferred_element_type=f32) * scale
+        sc = sc + jnp.where(positions < len_ref[i], 0.0, -1e30)
+        peak = jnp.maximum(jnp.max(sc, axis=-1, keepdims=True), -1e29)
         peak = jnp.where(leading, jnp.maximum(peak, fresh), peak)
-        w = jnp.where(in_range, jnp.exp(sc - peak), 0.0)
+        w = jnp.exp(sc - peak)
         wn = jnp.where(leading, jnp.exp(fresh - peak), 0.0)
         norm = jnp.sum(w, axis=-1, keepdims=True) + wn
         both = jnp.broadcast_to(jnp.concatenate([peak, norm], axis=0), (2 * QUERY_HEADS, 128))
         stat_buf[f, i] = both.T[0:8, :]
         v_copy(i).wait()
         o = jnp.dot(w.astype(bf16), v_v[i], preferred_element_type=f32)
-        o = o + wn.astype(bf16).astype(f32) * dv_ref[i : i + 1, :].astype(f32)
-        o = jnp.where(diag, o, 0.0)
-        part = o[:, :HEAD_WIDTH]
-        for b in range(1, KEY_VALUE_HEADS):
-            part = part + o[:, b * HEAD_WIDTH : (b + 1) * HEAD_WIDTH]
-        acc_buf[f, i] = part.astype(bf16)
+        wn = wn.astype(bf16).astype(f32)
+        acc_buf[f, i] = jnp.concatenate(
+            [o[at, lanes] + wn[at] * dv_ref[i : i + 1, lanes].astype(f32) for at, lanes in heads],
+            axis=0,
+        ).astype(bf16)
         if i == 0:
             pl.semaphore_wait(barrier, group - 1)
 
@@ -289,9 +292,10 @@
         attended = turned[:QUERY_HEADS, 0:1] * acc_buf[0, i].astype(f32)
         for z in range(1, F):
             attended = attended + turned[:QUERY_HEADS, 8 * z : 8 * z + 1] * acc_buf[z, i].astype(f32)
-        for h in range(QUERY_HEADS):
-            att_row[i : i + 1, h * HEAD_WIDTH : (h + 1) * HEAD_WIDTH] = attended[h : h + 1, :]
-        att_buf[mine, i] = att_row[i : i + 1, :].astype(bf16)
+        att_rows[...] = attended
+        att_buf[mine, i] = jnp.concatenate(
+            [att_rows[h : h + 1, :] for h in range(QUERY_HEADS)], axis=1
+        ).astype(bf16)
 
         def send_att(t, c, i=i):
             att_copy(lax.rem(mine + t, SR), mine, i).start()
@@ -301,17 +305,12 @@
 
     turn_range(*TURNS[1])
 
-    def recv_att(t, c):
-        src = lax.rem(mine + t, SR)
+    for t in range(SR):
+        src = lax.rem(mine + t * R + t * R // SR, SR)
         for i in range(rows_q):
-            att_copy(src, src, i).wait_recv()
-        return c
-
-    lax.fori_loop(1, SR, recv_att, 0)
-    for j in range(SR):
-        for i in range(rows_q):
-            at = j * rows_q + i
-            att_full[at : at + 1, :] = att_buf[j, i].astype(f32)
+            if t > 0:
+                att_copy(src, src, i).wait_recv()
+            att_full[pl.ds(src * rows_q + i, 1), :] = att_buf[src, i].astype(f32)
     for copy in small[4:]:
         copy.wait()
     proj = res_ref[...].astype(f32)
@@ -414,9 +413,7 @@
         sib_send[ffn, :, pair:] = split(squares)
         sib_copy(j).start()
 
-    def project_far(j):
-        _, ffn, p = block(1, j)
-        v = project(p)
+    def project_far(j, ffn, v):
         sib_copy(j).wait_recv()
         gu_send[ffn, :, :pair] = (v + sib_recv[ffn, :, :pair].astype(f32)).astype(bf16)
         gu_send[ffn, :, pair:] = split(squares + joined(sib_recv[ffn, :, pair:]))
@@ -424,9 +421,15 @@
 
     def project_both(j, c):
         wait_raw(2 * j + 1)
-        project_sibling(j + 1)
         wait_raw(2 * j + 2)
-        project_far(j)
+        _, sib, p = block(0, j + 1)
+        _, ffn, q = block(1, j)
+        a = project(p)
+        v = project(q)
+        sib_send[sib, :, :pair] = a.astype(bf16)
+        sib_send[sib, :, pair:] = split(squares)
+        sib_copy(j + 1).start()
+        project_far(j, ffn, v)
         return c
 
     wait_raw(0)
@@ -589,10 +592,11 @@
             pltpu.VMEM((OUT_CHUNKS, out_rows, cols), bf16),
             pltpu.VMEM((PN, *turned), bf16),
             pltpu.VMEM((PN, unit, seg_cols), bf16),
-            pltpu.VMEM((rows_q, QUERY_HEADS, kv_width), f32),
+            pltpu.VMEM((rows_q, QUERY_HEADS, HEAD_WIDTH), f32),
+            pltpu.VMEM((rows_q, QUERY_HEADS, kv_width), bf16),
             pltpu.VMEM((F, rows_q, QUERY_HEADS, HEAD_WIDTH), bf16),
             pltpu.VMEM((F, rows_q, 8, 128), f32),
-            pltpu.VMEM((rows_q, QUERY_HEADS * HEAD_WIDTH), f32),
+            pltpu.VMEM((QUERY_HEADS, HEAD_WIDTH), f32),
             pltpu.VMEM((SR, rows_q, 1, QUERY_HEADS * HEAD_WIDTH), bf16),
             pltpu.VMEM((total_rows, QUERY_HEADS * HEAD_WIDTH), f32),
             pltpu.VMEM((R, total_rows, pl.cdiv(cols, 128) * 128 + 128), bf16),

time: 38.1 us -> 37.3 us (0.979)
  Pallas kernels: 37.3 us -> 36.5 us
    pallas_call x1, Pallas kernels: 37.3 us -> 36.5 us  [body(): pl.pallas_call(functools.partial(kernel, S, F, R), out_shape=pltpu.VMEM((...]
where the time goes in v3:
time: 37.3 us; the launch traced here: 37.2 us
  Pallas kernels  36.5 us (98%)
  local copies, waits for them, and re-layouts  0.6 us (2%)
    pallas_call x1, Pallas kernels, body(): pl.pallas_call(functools.partial(kernel, S, F, R), out_shape=pltpu.VMEM((...  36.5 us

profile of v3, /device:TPU:0, one launch (start us, length us, event | category | flops | bytes accessed | tf_op | source)
XLA Modules:
  0.0 37.2 jit_solution(15694725433694135848)
XLA Ops:
  0.0 36.5 %decode_step.1 = bf16[8,512]{1,0:T(8,128)(2,1)S(1)} custom-call(bf16[2,8192]{1,0:T(2,128)(2,1)} %q_hbm.1, bf16[2,1024]{1,0:T(2,128)(2,1)} %dk_hbm.1, bf16[2,1024]{1,0:T(2,128)(2,1)} %dv_hbm.1, s32[2]{0:T(128)} %len_hbm.1, s32[4]{0:T(128)} %cnt_hbm.1, bf16[8,512]{1,0:T(8,128)(2,1)} %res_hbm.1, bf16[512]{0:T(512)(128)(2,1)} %gain_hbm.1, ...), custom_call_target="tpu_custom_call" | custom-call | tf_op jit(solution)/shard_map/decode_step/pallas_call | solution.py:580
  36.5 0.6 %copy.15 = bf16[8,512]{1,0:T(8,128)(2,1)} copy(bf16[8,512]{1,0:T(8,128)(2,1)S(1)} %decode_step.1) | data formatting | bytes 16384

commit v4 on v3

--- a/solution.py
+++ b/solution.py
@@ -83,13 +83,18 @@
     def wd_copy(p):
         return pltpu.make_async_copy(wd_hbm.at[unit_rows(p)], wd_v.at[p], wd_sem.at[p])
 
+    flip = lax.div(2 * f, F)
+
     def line(j):
-        flip = 2 * f // F
-        up = j + (j - f + F) // F
         v = F - 1 - j
-        down = v - (f - v + F) // F
-        last = (j + 1) // F
+        up = j + lax.div(j - f + F, F)
+        down = v - lax.div(f - v + F, F)
+        if isinstance(j, int):
+            return f if j == F - 1 else flip * up + (1 - flip) * down
+        last = lax.div(j + 1, F)
         return (1 - last) * (flip * up + (1 - flip) * down) + last * f
+
+    lines = [line(j) for j in range(F)]
 
     def block(own, j):
         side = own * s + (1 - own) * (S - 1 - s)
@@ -97,9 +102,10 @@
         return side, ffn, side * F + ffn
 
     def in_turn(q):
-        last = (q + 1) // PN
-        own = (1 - lax.rem(q, 2)) * ((q + PN - 1) // PN) + last
-        return block(own, own * (q // 2 - 1 + last) + (1 - own) * ((q + 1) // 2))
+        last = lax.div(q + 1, PN)
+        own = (1 - lax.rem(q, 2)) * lax.div(q + PN - 1, PN) + last
+        half = lax.div(q, 2)
+        return block(own, own * (half - 1 + last) + (1 - own) * (half + lax.rem(q, 2)))
 
     def raw_copy(m, t):
         _, _, p = in_turn(t)
@@ -133,13 +139,14 @@
             lax.fori_loop(lo * PN // 8, min(hi * PN // 8, PN - 1), turn_pair, 0)
 
     def far_first(t):
-        last = t // (PN - 2)
-        side = (1 - last) * lax.rem(t, 2) + last * (S - 1 - s)
-        ffn = line(t // 2)
+        side = S - 1 - s if t == PN - 2 else t % 2
+        ffn = lines[t // 2]
         return side, ffn, side * F + ffn
 
     def near_first(t):
-        return block(1 - lax.rem(t, 2), F - 1 - t // 2)
+        side = s if t % 2 == 0 else S - 1 - s
+        ffn = lines[F - 1 - t // 2]
+        return side, ffn, side * F + ffn
 
     small = [
         pltpu.make_async_copy(src, dst, small_sem.at[n])
@@ -252,12 +259,8 @@
         lax.fori_loop(1, F, send_acc, 0)
 
     if not turn:
-        def start_down(t, c):
-            _, _, p = near_first(t)
-            wd_copy(p).start(priority=1)
-            return c
-
-        lax.fori_loop(0, PN, start_down, 0)
+        for t in range(PN):
+            wd_copy(near_first(t)[2]).start(priority=1)
 
     turn_range(*TURNS[0])
 
@@ -305,6 +308,8 @@
 
     turn_range(*TURNS[1])
 
+    for i in range(OUT_CHUNKS):
+        wo_copy(i).wait()
     for t in range(SR):
         src = lax.rem(mine + t * R + t * R // SR, SR)
         for i in range(rows_q):
@@ -316,7 +321,6 @@
     proj = res_ref[...].astype(f32)
     summed = jnp.zeros((total_rows, cols), f32)
     for i in range(OUT_CHUNKS):
-        wo_copy(i).wait()
         summed = summed + jnp.dot(
             att_full[:, i * out_rows : (i + 1) * out_rows].astype(bf16),
             wo_v[i],
@@ -452,36 +456,54 @@
     sums = sums + sib_recv[f, :, :pair].astype(f32)
     squares = squares + joined(sib_recv[f, :, pair:])
 
-    def gather_sums(t, c):
-        src = line(F - 1 - t)
+    for t in range(1, F):
+        src = lines[F - 1 - t]
         gu_copy(src, False).wait_recv()
         v = gu_recv[src]
-        return c[0] + v[:, :pair].astype(f32), c[1] + joined(v[:, pair:])
-
-    sums, squares = lax.fori_loop(1, F, gather_sums, (sums, squares))
+        sums = sums + v[:, :pair].astype(f32)
+        squares = squares + joined(v[:, pair:])
+
     sums = sums * lax.rsqrt(squares / D + norm_eps)[:, 0:1]
     g = sums[:, :unit]
     u = sums[:, up_at : up_at + unit]
     hid[me] = (g / (1.0 + jnp.exp(-g)) * u).astype(bf16)
 
-    def send_hid(t, c):
+    for t in range(PN - 1):
         hid_copy(t, True).start()
-        return c
-
-    lax.fori_loop(0, PN - 1, send_hid, 0)
-
-    def down(t, c):
-        _, _, p = near_first(t)
+
+    def drain_f(t, c):
+        to = lax.rem(f + t, F)
+        for i in range(rows_q):
+            stat_copy(to, f, i).wait_send()
+            acc_copy(to, f, i).wait_send()
+        gu_copy(to, True).wait_send()
+        return c
+
+    lax.fori_loop(1, F, drain_f, 0)
+
+    def drain_sr(t, c):
+        for i in range(rows_q):
+            att_copy(lax.rem(mine + t, SR), mine, i).wait_send()
+        return c
+
+    lax.fori_loop(1, SR, drain_sr, 0)
+
+    def drain_y(t, c):
+        y_copy(lax.rem(r + t, R), r).wait_send()
+        return c
+
+    lax.fori_loop(1, R, drain_y, 0)
+
+    for j in range(F):
+        sib_copy(j).wait_send()
+
+    terms = jnp.zeros((total_rows, seg_cols), f32)
+    for t in range(PN):
+        p = near_first(t)[2]
         wd_copy(p).wait()
-
-        @pl.when(t > 0)
-        def _():
+        if t > 0:
             hid_copy(t, False).wait_recv()
-
-        return c + jnp.dot(hid[p], wd_v[p], preferred_element_type=f32)
-
-    terms = jnp.zeros((total_rows, seg_cols), f32)
-    terms = lax.fori_loop(0, PN, down, terms, unroll=True)
+        terms = terms + jnp.dot(hid[p], wd_v[p], preferred_element_type=f32)
     terms = terms.astype(bf16)
     for j in range(R):
         if aligned:
@@ -510,6 +532,9 @@
         limit = jnp.where(row // slots == i, cnt_ref[i], limit)
     active = lax.rem(row, slots) < limit
 
+    for t in range(PN - 1):
+        hid_copy(t, True).wait_send()
+
     def recv_d(t, c):
         src = lax.rem(r + t, R)
         d_copy(src, False).wait_recv()
@@ -518,47 +543,11 @@
     ffn_out = lax.fori_loop(1, R, recv_d, d_send[r].astype(f32))
     out_ref[...] = jnp.where(active, stream + ffn_out, 0.0).astype(bf16)
 
-    def drain_f(t, c):
-        to = lax.rem(f + t, F)
-        for i in range(rows_q):
-            stat_copy(to, f, i).wait_send()
-            acc_copy(to, f, i).wait_send()
-        return c
-
-    lax.fori_loop(1, F, drain_f, 0)
-
-    def drain_sr(t, c):
-        for i in range(rows_q):
-            att_copy(lax.rem(mine + t, SR), mine, i).wait_send()
-        return c
-
-    lax.fori_loop(1, SR, drain_sr, 0)
-
-    def drain_r(t, c):
-        to = lax.rem(r + t, R)
-        y_copy(to, r).wait_send()
-        d_copy(to, True).wait_send()
-        return c
-
-    lax.fori_loop(1, R, drain_r, 0)
-
-    def drain_p(t, c):
-        hid_copy(t, True).wait_send()
-        return c
-
-    lax.fori_loop(0, PN - 1, drain_p, 0)
-
-    def drain_sibling(j, c):
-        sib_copy(j).wait_send()
-        return c
-
-    lax.fori_loop(0, F, drain_sibling, 0)
-
-    def drain_gu(t, c):
-        gu_copy(lax.rem(f + t, F), True).wait_send()
-        return c
-
-    lax.fori_loop(1, F, drain_gu, 0)
+    def drain_d(t, c):
+        d_copy(lax.rem(r + t, R), True).wait_send()
+        return c
+
+    lax.fori_loop(1, R, drain_d, 0)
 
 
 def body(S, F, R, queries, key_cache, value_cache, decoded_key, decoded_value, lengths, counts,

time: 37.3 us -> 36.3 us (0.973)
  Pallas kernels: 36.5 us -> 35.5 us
    pallas_call x1, Pallas kernels: 36.5 us -> 35.5 us  [body(): pl.pallas_call(functools.partial(kernel, S, F, R), out_shape=pltpu.VMEM((...]
where the time goes in v4:
time: 36.3 us; the launch traced here: 36.1 us
  Pallas kernels  35.5 us (98%)
  local copies, waits for them, and re-layouts  0.6 us (2%)
    pallas_call x1, Pallas kernels, body(): pl.pallas_call(functools.partial(kernel, S, F, R), out_shape=pltpu.VMEM((...  35.5 us

profile of v4, /device:TPU:0, one launch (start us, length us, event | category | flops | bytes accessed | tf_op | source)
XLA Modules:
  0.0 36.1 jit_solution(8192149081975261786)
XLA Ops:
  0.0 35.5 %decode_step.1 = bf16[8,512]{1,0:T(8,128)(2,1)S(1)} custom-call(bf16[2,8192]{1,0:T(2,128)(2,1)} %q_hbm.1, bf16[2,1024]{1,0:T(2,128)(2,1)} %dk_hbm.1, bf16[2,1024]{1,0:T(2,128)(2,1)} %dv_hbm.1, s32[2]{0:T(128)} %len_hbm.1, s32[4]{0:T(128)} %cnt_hbm.1, bf16[8,512]{1,0:T(8,128)(2,1)} %res_hbm.1, bf16[512]{0:T(512)(128)(2,1)} %gain_hbm.1, ...), custom_call_target="tpu_custom_call" | custom-call | tf_op jit(solution)/shard_map/decode_step/pallas_call | solution.py:569
  35.5 0.6 %copy.15 = bf16[8,512]{1,0:T(8,128)(2,1)} copy(bf16[8,512]{1,0:T(8,128)(2,1)S(1)} %decode_step.1) | data formatting | bytes 16384

commit v5 on v4

--- a/solution.py
+++ b/solution.py
@@ -15,7 +15,7 @@
 OUT_CHUNKS = 4
 TURN_COLS = 256
 WO_AT = 2
-TURNS = ((0, 2), (2, 5), (5, 7))
+TURNS = ((0, 2), (2, 4), (4, 6))
 
 norm_eps = 1e-05
 MESH = pl.DeviceIdType.MESH
@@ -102,6 +102,7 @@
         return side, ffn, side * F + ffn
 
     def in_turn(q):
+        q = q + lax.div(q + 3, PN) - 2 * lax.div(q + 2, PN) + lax.div(q + 1, PN)
         last = lax.div(q + 1, PN)
         own = (1 - lax.rem(q, 2)) * lax.div(q + PN - 1, PN) + last
         half = lax.div(q, 2)
@@ -136,7 +137,7 @@
 
     def turn_range(lo, hi):
         if turn:
-            lax.fori_loop(lo * PN // 8, min(hi * PN // 8, PN - 1), turn_pair, 0)
+            lax.fori_loop(lo * PN // 8, min(hi * PN // 8, PN - 2), turn_pair, 0)
 
     def far_first(t):
         side = S - 1 - s if t == PN - 2 else t % 2
@@ -159,9 +160,9 @@
     k_copy(0).start()
     for copy in small[1:4]:
         copy.start()
+    v_copy(0).start()
     for i in range(1, rows_q):
         k_copy(i).start()
-    for i in range(rows_q):
         v_copy(i).start()
     for copy in small[4:]:
         copy.start()
@@ -174,7 +175,7 @@
         pl.semaphore_signal(
             barrier,
             inc=1,
-            device_id=dev(other // (F * R), lax.rem(other // R, F), lax.rem(other, R)),
+            device_id=dev(lax.div(other, F * R), lax.rem(lax.div(other, R), F), lax.rem(other, R)),
             device_id_type=MESH,
         )
         return c
@@ -267,7 +268,7 @@
     def att_copy(other, slot, i):
         return remote(
             att_buf.at[slot, i], att_buf.at[slot, i], att_ss.at[other, i], att_rs.at[slot, i],
-            dev(other // R, f, lax.rem(other, R)),
+            dev(lax.div(other, R), f, lax.rem(other, R)),
         )
 
     low = lax.broadcasted_iota(jnp.int32, (8, 128), 1) < QUERY_HEADS
@@ -411,9 +412,22 @@
             raw_copy(0, q).wait()
             raw_copy(1, q).wait()
 
-    def project_sibling(j):
-        _, ffn, p = block(0, j)
-        sib_send[ffn, :, :pair] = project(p).astype(bf16)
+    def project_stored(q, p):
+        if not turn:
+            wait_raw(q)
+            return project(p)
+        both = []
+        for m in range(2):
+            at = 2 * (q % ahead) + m
+            raw_copy(m, q).wait()
+            both.append(lax.dot_general(segment, wd_v[at], NT, preferred_element_type=f32))
+        for m in range(2):
+            wd_copy(2 * (q % ahead) + m).start(priority=1)
+        return jnp.concatenate(both, axis=1)
+
+    def send_sibling(j, v):
+        ffn = lines[j]
+        sib_send[ffn, :, :pair] = v.astype(bf16)
         sib_send[ffn, :, pair:] = split(squares)
         sib_copy(j).start()
 
@@ -437,21 +451,13 @@
         return c
 
     wait_raw(0)
-    project_sibling(0)
-    lax.fori_loop(0, F - 1, project_both, 0)
-    if turn:
-        sums = []
-        for m in range(2):
-            at = 2 * lax.rem(PN - 1, ahead) + m
-            raw_copy(m, PN - 1).wait()
-            sums.append(
-                lax.dot_general(segment, wd_v[at], NT, preferred_element_type=f32)
-            )
-            wd_copy(at).start(priority=1)
-        sums = jnp.concatenate(sums, axis=1)
-    else:
-        wait_raw(PN - 1)
-        sums = project(me)
+    send_sibling(0, project(block(0, 0)[2]))
+    lax.fori_loop(0, F - 2, project_both, 0)
+    wait_raw(PN - 3)
+    _, near, at_near = block(1, F - 2)
+    project_far(F - 2, near, project(at_near))
+    send_sibling(F - 1, project_stored(PN - 2, block(0, F - 1)[2]))
+    sums = project_stored(PN - 1, me)
     sib_copy(F - 1).wait_recv()
     sums = sums + sib_recv[f, :, :pair].astype(f32)
     squares = squares + joined(sib_recv[f, :, pair:])

time: 36.3 us -> 35.7 us (0.983)
  Pallas kernels: 35.5 us -> 34.9 us
    pallas_call x1, Pallas kernels: 35.5 us -> 34.9 us  [body(): pl.pallas_call(functools.partial(kernel, S, F, R), out_shape=pltpu.VMEM((...]
where the time goes in v5:
time: 35.7 us; the launch traced here: 35.5 us
  Pallas kernels  34.9 us (98%)
  local copies, waits for them, and re-layouts  0.6 us (2%)
    pallas_call x1, Pallas kernels, body(): pl.pallas_call(functools.partial(kernel, S, F, R), out_shape=pltpu.VMEM((...  34.9 us

profile of v5, /device:TPU:0, one launch (start us, length us, event | category | flops | bytes accessed | tf_op | source)
XLA Modules:
  0.0 35.5 jit_solution(1184558188350757737)
XLA Ops:
  0.0 34.9 %decode_step.1 = bf16[8,512]{1,0:T(8,128)(2,1)S(1)} custom-call(bf16[2,8192]{1,0:T(2,128)(2,1)} %q_hbm.1, bf16[2,1024]{1,0:T(2,128)(2,1)} %dk_hbm.1, bf16[2,1024]{1,0:T(2,128)(2,1)} %dv_hbm.1, s32[2]{0:T(128)} %len_hbm.1, s32[4]{0:T(128)} %cnt_hbm.1, bf16[8,512]{1,0:T(8,128)(2,1)} %res_hbm.1, bf16[512]{0:T(512)(128)(2,1)} %gain_hbm.1, ...), custom_call_target="tpu_custom_call" | custom-call | tf_op jit(solution)/shard_map/decode_step/pallas_call | solution.py:575
  34.9 0.6 %copy.15 = bf16[8,512]{1,0:T(8,128)(2,1)} copy(bf16[8,512]{1,0:T(8,128)(2,1)S(1)} %decode_step.1) | data formatting | bytes 16384

commit v6 on v5

--- a/solution.py
+++ b/solution.py
@@ -32,7 +32,7 @@
     q_ref, dk_ref, dv_ref, len_ref, cnt_ref, res_ref, gain_ref,
     k_v, v_v, wo_v, wt_v, wd_v,
     q_rows, qbd, acc_buf, stat_buf, att_rows, att_buf, att_full,
-    y_buf,
+    y_buf, pre,
     sib_send, sib_recv, gu_send, gu_recv, hid, d_send, d_recv,
     small_sem, k_sem, v_sem, wo_sem, raw_sem, wd_sem,
     acc_ss, acc_rs, stat_ss, stat_rs, att_ss, att_rs,
@@ -356,6 +356,22 @@
 
     aligned = cols % 128 == 0
     turn_range(*TURNS[2])
+    early = turn and aligned and R == 2 and cols % 256 == 0
+
+    def half_of(which, lhs):
+        return sum(
+            jnp.dot(
+                lhs[:, at : at + 256],
+                wt_v[
+                    block(0, 0)[2], pl.ds(pl.multiple_of(which * cols + at, 256), 256)
+                ],
+                preferred_element_type=f32,
+            )
+            for at in range(0, cols, 256)
+        )
+
+    if early:
+        pre[...] = half_of(r, y_buf[r, :, :cols])
 
     def recv_y(t, c):
         src = lax.rem(r + t, R)
@@ -451,7 +467,10 @@
         return c
 
     wait_raw(0)
-    send_sibling(0, project(block(0, 0)[2]))
+    if early:
+        send_sibling(0, pre[...] + half_of(1 - r, y_buf[1 - r, :, :cols]))
+    else:
+        send_sibling(0, project(block(0, 0)[2]))
     lax.fori_loop(0, F - 2, project_both, 0)
     wait_raw(PN - 3)
     _, near, at_near = block(1, F - 2)
@@ -595,6 +614,7 @@
             pltpu.VMEM((SR, rows_q, 1, QUERY_HEADS * HEAD_WIDTH), bf16),
             pltpu.VMEM((total_rows, QUERY_HEADS * HEAD_WIDTH), f32),
             pltpu.VMEM((R, total_rows, pl.cdiv(cols, 128) * 128 + 128), bf16),
+            pltpu.VMEM((total_rows, pair), f32),
             *[pltpu.VMEM((F, total_rows, pair + 128), bf16) for _ in range(4)],
             pltpu.VMEM((PN, total_rows, unit), bf16),
             pltpu.VMEM((R, total_rows, cols), bf16),

time: 35.7 us -> 35.4 us (level)
  no operation moved by 1% of the time
where the time goes in v6:
time: 35.4 us; the launch traced here: 35.3 us
  Pallas kernels  34.6 us (98%)
  local copies, waits for them, and re-layouts  0.6 us (2%)
    pallas_call x1, Pallas kernels, body(): pl.pallas_call(functools.partial(kernel, S, F, R), out_shape=pltpu.VMEM((...  34.6 us

profile of v6, /device:TPU:0, one launch (start us, length us, event | category | flops | bytes accessed | tf_op | source)
XLA Modules:
  0.0 35.3 jit_solution(9728329366942506401)
XLA Ops:
  0.0 34.6 %decode_step.1 = bf16[8,512]{1,0:T(8,128)(2,1)S(1)} custom-call(bf16[2,8192]{1,0:T(2,128)(2,1)} %q_hbm.1, bf16[2,1024]{1,0:T(2,128)(2,1)} %dk_hbm.1, bf16[2,1024]{1,0:T(2,128)(2,1)} %dv_hbm.1, s32[2]{0:T(128)} %len_hbm.1, s32[4]{0:T(128)} %cnt_hbm.1, bf16[8,512]{1,0:T(8,128)(2,1)} %res_hbm.1, bf16[512]{0:T(512)(128)(2,1)} %gain_hbm.1, ...), custom_call_target="tpu_custom_call" | custom-call | tf_op jit(solution)/shard_map/decode_step/pallas_call | solution.py:594
  34.6 0.6 %copy.15 = bf16[8,512]{1,0:T(8,128)(2,1)} copy(bf16[8,512]{1,0:T(8,128)(2,1)S(1)} %decode_step.1) | data formatting | bytes 16384
